TPU v7x, 128 devices: a whole 4x4x4 slice. The times are simulated.
128 devices in a mesh: ctx: 32 (over y, z, x_lo), seq: 2 (over core), fsdp: 2 (over x_hi).
Axes of the slice: x: 4 (x_hi: 2, x_lo: 2; x = x_hi * 2 + x_lo), y: 4, z: 4, core: 2. Of those that a mesh axis runs over, the one named last changes fastest.
Arguments:
- tokens: bfloat16 [4, 4096, 768], P(('seq', 'fsdp'), 'ctx'), may hold values from -6 to 6
- cotangent: bfloat16 [4, 4096, 768], P(('seq', 'fsdp'), 'ctx'), may hold values from -6 to 6
- w_query: bfloat16 [768, 768], P('fsdp'), may hold values from -0.21875 to 0.21875
- w_key: bfloat16 [768, 768], P('fsdp'), may hold values from -0.21875 to 0.21875
- w_value: bfloat16 [768, 768], P('fsdp'), may hold values from -0.21875 to 0.21875
- w_output: bfloat16 [768, 768], P('fsdp'), may hold values from -6 to 6
- b_query: bfloat16 [768], P('fsdp'), may hold values from -1.5 to 1.5
- b_value: bfloat16 [768], P('fsdp'), may hold values from -0.15625 to 0.15625
- b_output: bfloat16 [768], P('fsdp'), may hold values from -1.5 to 1.5
- first_gain: bfloat16 [768], P('fsdp'), may hold values from 0.5 to 1.5
- first_shift: bfloat16 [768], P('fsdp'), may hold values from -1.5 to 1.5
- w_inner: bfloat16 [768, 3072], P('fsdp'), may hold values from -0.21875 to 0.21875
- b_inner: bfloat16 [3072], P('fsdp'), may hold values from -1.5 to 1.5
- w_outer: bfloat16 [3072, 768], P('fsdp'), may hold values from -0.109375 to 0.109375
- b_outer: bfloat16 [768], P('fsdp'), may hold values from -1.5 to 1.5
- second_gain: bfloat16 [768], P('fsdp'), may hold values from 0.5 to 1.5
- second_shift: bfloat16 [768], P('fsdp'), may hold values from -1.5 to 1.5
Outputs:
- layer_out: bfloat16 [4, 4096, 768], P(('seq', 'fsdp'), 'ctx')
- tokens_grad: float32 [4, 4096, 768], P(('seq', 'fsdp'), 'ctx')
- w_query_grad: float32 [768, 768], P('fsdp')
- w_key_grad: float32 [768, 768], P('fsdp')
- w_value_grad: float32 [768, 768], P('fsdp')
- w_output_grad: float32 [768, 768], P('fsdp')
- b_query_grad: float32 [768], P('fsdp')
- b_value_grad: float32 [768], P('fsdp')
- b_output_grad: float32 [768], P('fsdp')
- first_gain_grad: float32 [768], P('fsdp')
- first_shift_grad: float32 [768], P('fsdp')
- w_inner_grad: float32 [768, 3072], P('fsdp')
- b_inner_grad: float32 [3072], P('fsdp')
- w_outer_grad: float32 [3072, 768], P('fsdp')
- b_outer_grad: float32 [768], P('fsdp')
- second_gain_grad: float32 [768], P('fsdp')
- second_shift_grad: float32 [768], P('fsdp')
All inputs are finite; a program needn't handle non-finite values.
Results may differ from a plain program's by a relative error of at most 0.022.
Values may be sent and summed in bfloat16 or wider, within the bound.
A program may use at most 192 MiB of HBM per device.

v0:
```python
import functools
import jax
import jax.numpy as jnp
from jax import lax
from jax.sharding import PartitionSpec as P

HEADS = 12
HEAD_DIM = 64
epsilon = 1e-12


def product(left, right):
    return jnp.dot(left, right, preferred_element_type=jnp.float32)


def product_left(left, right):
    return lax.dot_general(
        left, right, (((0,), (0,)), ((), ())), preferred_element_type=jnp.float32
    )


def product_right(left, right):
    return lax.dot_general(
        left, right, (((1,), (1,)), ((), ())), preferred_element_type=jnp.float32
    )


def layer_norm(hidden, gain, shift):
    centred = hidden - jnp.mean(hidden, axis=-1, keepdims=True)
    inverse = lax.rsqrt(jnp.mean(centred * centred, axis=-1, keepdims=True) + epsilon)
    normal = centred * inverse
    return (normal * gain + shift, normal, inverse)


def norm_back(grad, normal, inverse, gain):
    scaled = grad * gain
    centre = jnp.mean(scaled, axis=-1, keepdims=True)
    along = jnp.mean(scaled * normal, axis=-1, keepdims=True)
    return inverse * (scaled - centre - normal * along)


def group_slice(array, index):
    columns = 2 * HEAD_DIM
    piece = lax.dynamic_slice_in_dim(array, index * columns, columns, 2)
    return piece.reshape(piece.shape[0], piece.shape[1], 2, HEAD_DIM)


def scores_of(query, keys):
    return jnp.einsum(
        "sqhd,skhd->shqk", query, keys, preferred_element_type=jnp.float32
    ) * HEAD_DIM ** (-0.5)


def flatten_group(array):
    return array.reshape(array.shape[0], array.shape[1], 2 * HEAD_DIM)


def to_rows(stacked):
    groups, seqs, count, columns = stacked.shape
    return stacked.transpose(1, 2, 0, 3).reshape(seqs * count, groups * columns)


def local(
    tokens,
    cotangent,
    w_query,
    w_key,
    w_value,
    w_output,
    b_query,
    b_value,
    b_output,
    first_gain,
    first_shift,
    w_inner,
    b_inner,
    w_outer,
    b_outer,
    second_gain,
    second_shift,
):
    seqs, block, width = tokens.shape
    rows = seqs * block
    indices = jnp.arange(HEADS // 2)
    scale = HEAD_DIM ** (-0.5)
    w_query, w_key, w_value, w_output, b_query, b_value, b_output, first_gain, first_shift = (
        lax.all_gather(w_query, "fsdp", axis=0, tiled=True),
        lax.all_gather(w_key, "fsdp", axis=0, tiled=True),
        lax.all_gather(w_value, "fsdp", axis=0, tiled=True),
        lax.all_gather(w_output, "fsdp", axis=0, tiled=True),
        lax.all_gather(b_query, "fsdp", axis=0, tiled=True),
        lax.all_gather(b_value, "fsdp", axis=0, tiled=True),
        lax.all_gather(b_output, "fsdp", axis=0, tiled=True),
        lax.all_gather(first_gain, "fsdp", axis=0, tiled=True),
        lax.all_gather(first_shift, "fsdp", axis=0, tiled=True),
    )
    flat = tokens.reshape(rows, width)
    query = (product(flat, w_query) + b_query).astype(jnp.bfloat16).reshape(seqs, block, width)
    keys = product(flat, w_key).astype(jnp.bfloat16).reshape(seqs, block, width)
    values = (product(flat, w_value) + b_value).astype(jnp.bfloat16).reshape(seqs, block, width)
    keys_all, values_all = (
        lax.all_gather(keys, "ctx", axis=1, tiled=True),
        lax.all_gather(values, "ctx", axis=1, tiled=True),
    )

    def forward_group(index):
        scores = scores_of(group_slice(query, index), group_slice(keys_all, index))
        top = jnp.max(scores, axis=-1, keepdims=True)
        weights = jnp.exp(scores - top)
        total = jnp.sum(weights, axis=-1, keepdims=True)
        probs = (weights / total).astype(jnp.bfloat16)
        mixed = jnp.einsum(
            "shqk,skhd->sqhd",
            probs,
            group_slice(values_all, index),
            preferred_element_type=jnp.float32,
        )
        return (flatten_group(mixed), (top + jnp.log(total))[..., 0])

    mixed, logsum = lax.map(forward_group, indices)
    attended = to_rows(mixed).astype(jnp.bfloat16)
    first_in = flat.astype(jnp.float32) + product(attended, w_output) + b_output
    normed, first_normal, first_inverse = layer_norm(first_in, first_gain, first_shift)
    normed_low = normed.astype(jnp.bfloat16)
    w_inner, b_inner, w_outer, b_outer, second_gain, second_shift = (
        lax.all_gather(w_inner, "fsdp", axis=0, tiled=True),
        lax.all_gather(b_inner, "fsdp", axis=0, tiled=True),
        lax.all_gather(w_outer, "fsdp", axis=0, tiled=True),
        lax.all_gather(b_outer, "fsdp", axis=0, tiled=True),
        lax.all_gather(second_gain, "fsdp", axis=0, tiled=True),
        lax.all_gather(second_shift, "fsdp", axis=0, tiled=True),
    )
    gelu_exact = functools.partial(jax.nn.gelu, approximate=False)
    inner = product(normed_low, w_inner) + b_inner
    active = gelu_exact(inner).astype(jnp.bfloat16)
    second_in = normed + product(active, w_outer) + b_outer
    layer_out, second_normal, second_inverse = layer_norm(second_in, second_gain, second_shift)
    grad_out = cotangent.reshape(rows, width).astype(jnp.float32)
    second_scale = jnp.sum(grad_out * second_normal, axis=0)
    second_offset = jnp.sum(grad_out, axis=0)
    grad_second = norm_back(grad_out, second_normal, second_inverse, second_gain)
    outer_low = grad_second.astype(jnp.bfloat16)
    outer_matrix = product_left(active, outer_low)
    outer_bias = jnp.sum(outer_low.astype(jnp.float32), axis=0)
    slope = jax.vjp(gelu_exact, inner)[1](product_right(outer_low, w_outer))[0]
    inner_low = slope.astype(jnp.bfloat16)
    inner_matrix = product_left(normed_low, inner_low)
    inner_bias = jnp.sum(inner_low.astype(jnp.float32), axis=0)
    grad_normed = grad_second + product_right(inner_low, w_inner)
    first_scale = jnp.sum(grad_normed * first_normal, axis=0)
    first_offset = jnp.sum(grad_normed, axis=0)
    grad_first = norm_back(grad_normed, first_normal, first_inverse, first_gain)
    branch_low = grad_first.astype(jnp.bfloat16)
    output_matrix = product_left(attended, branch_low)
    output_bias = jnp.sum(branch_low.astype(jnp.float32), axis=0)
    upstream = product_right(branch_low, w_output).astype(jnp.bfloat16).reshape(seqs, block, width)

    def backward_group(pair):
        index, group_logsum = pair
        query_part = group_slice(query, index)
        keys_part = group_slice(keys_all, index)
        values_part = group_slice(values_all, index)
        upstream_part = group_slice(upstream, index)
        probs = jnp.exp(scores_of(query_part, keys_part) - group_logsum[..., None])
        prob_grads = jnp.einsum(
            "sqhd,skhd->shqk", upstream_part, values_part, preferred_element_type=jnp.float32
        )
        row_dot = jnp.sum(probs * prob_grads, axis=-1, keepdims=True)
        score_low = (probs * (prob_grads - row_dot)).astype(jnp.bfloat16)
        query_grad = (
            jnp.einsum("shqk,skhd->sqhd", score_low, keys_part, preferred_element_type=jnp.float32)
            * scale
        )
        key_grad = (
            jnp.einsum("shqk,sqhd->skhd", score_low, query_part, preferred_element_type=jnp.float32)
            * scale
        )
        value_grad = jnp.einsum(
            "shqk,sqhd->skhd",
            probs.astype(jnp.bfloat16),
            upstream_part,
            preferred_element_type=jnp.float32,
        )
        return (flatten_group(query_grad), flatten_group(key_grad), flatten_group(value_grad))

    query_grads, key_terms, value_terms = lax.map(backward_group, (indices, logsum))
    key_grads, value_grads = (
        lax.psum_scatter(
            key_terms.astype(jnp.bfloat16), "ctx", scatter_dimension=2, tiled=True
        ).astype(jnp.float32),
        lax.psum_scatter(
            value_terms.astype(jnp.bfloat16), "ctx", scatter_dimension=2, tiled=True
        ).astype(jnp.float32),
    )
    query_low = to_rows(query_grads).astype(jnp.bfloat16)
    key_low = to_rows(key_grads).astype(jnp.bfloat16)
    value_low = to_rows(value_grads).astype(jnp.bfloat16)
    query_matrix = product_left(flat, query_low)
    query_bias = jnp.sum(query_low.astype(jnp.float32), axis=0)
    keys_matrix = product_left(flat, key_low)
    value_matrix = product_left(flat, value_low)
    value_bias = jnp.sum(value_low.astype(jnp.float32), axis=0)
    tokens_grad = (
        grad_first
        + product_right(query_low, w_query)
        + product_right(key_low, w_key)
        + product_right(value_low, w_value)
    )
    (
        query_matrix,
        keys_matrix,
        value_matrix,
        output_matrix,
        query_bias,
        value_bias,
        output_bias,
        first_scale,
        first_offset,
        inner_matrix,
        inner_bias,
        outer_matrix,
        outer_bias,
        second_scale,
        second_offset,
    ) = (
        lax.psum_scatter(
            query_matrix.astype(jnp.bfloat16), "fsdp", scatter_dimension=0, tiled=True
        ).astype(jnp.float32),
        lax.psum_scatter(
            keys_matrix.astype(jnp.bfloat16), "fsdp", scatter_dimension=0, tiled=True
        ).astype(jnp.float32),
        lax.psum_scatter(
            value_matrix.astype(jnp.bfloat16), "fsdp", scatter_dimension=0, tiled=True
        ).astype(jnp.float32),
        lax.psum_scatter(
            output_matrix.astype(jnp.bfloat16), "fsdp", scatter_dimension=0, tiled=True
        ).astype(jnp.float32),
        lax.psum_scatter(
            query_bias.astype(jnp.bfloat16), "fsdp", scatter_dimension=0, tiled=True
        ).astype(jnp.float32),
        lax.psum_scatter(
            value_bias.astype(jnp.bfloat16), "fsdp", scatter_dimension=0, tiled=True
        ).astype(jnp.float32),
        lax.psum_scatter(
            output_bias.astype(jnp.bfloat16), "fsdp", scatter_dimension=0, tiled=True
        ).astype(jnp.float32),
        lax.psum_scatter(
            first_scale.astype(jnp.bfloat16), "fsdp", scatter_dimension=0, tiled=True
        ).astype(jnp.float32),
        lax.psum_scatter(
            first_offset.astype(jnp.bfloat16), "fsdp", scatter_dimension=0, tiled=True
        ).astype(jnp.float32),
        lax.psum_scatter(
            inner_matrix.astype(jnp.bfloat16), "fsdp", scatter_dimension=0, tiled=True
        ).astype(jnp.float32),
        lax.psum_scatter(
            inner_bias.astype(jnp.bfloat16), "fsdp", scatter_dimension=0, tiled=True
        ).astype(jnp.float32),
        lax.psum_scatter(
            outer_matrix.astype(jnp.bfloat16), "fsdp", scatter_dimension=0, tiled=True
        ).astype(jnp.float32),
        lax.psum_scatter(
            outer_bias.astype(jnp.bfloat16), "fsdp", scatter_dimension=0, tiled=True
        ).astype(jnp.float32),
        lax.psum_scatter(
            second_scale.astype(jnp.bfloat16), "fsdp", scatter_dimension=0, tiled=True
        ).astype(jnp.float32),
        lax.psum_scatter(
            second_offset.astype(jnp.bfloat16), "fsdp", scatter_dimension=0, tiled=True
        ).astype(jnp.float32),
    )
    finals = lax.psum(
        (
            query_matrix,
            keys_matrix,
            value_matrix,
            output_matrix,
            query_bias,
            value_bias,
            output_bias,
            first_scale,
            first_offset,
            inner_matrix,
            inner_bias,
            outer_matrix,
            outer_bias,
            second_scale,
            second_offset,
        ),
        ("ctx", "seq"),
    )
    return (
        layer_out.astype(jnp.bfloat16).reshape(seqs, block, width),
        tokens_grad.reshape(seqs, block, width),
    ) + tuple(finals)


def solution(mesh):
    return jax.shard_map(
        local,
        mesh=mesh,
        in_specs=(
            P(("seq", "fsdp"), "ctx", None),
            P(("seq", "fsdp"), "ctx", None),
            P("fsdp", None),
            P("fsdp", None),
            P("fsdp", None),
            P("fsdp", None),
            P("fsdp"),
            P("fsdp"),
            P("fsdp"),
            P("fsdp"),
            P("fsdp"),
            P("fsdp", None),
            P("fsdp"),
            P("fsdp", None),
            P("fsdp"),
            P("fsdp"),
            P("fsdp"),
        ),
        out_specs=(
            P(("seq", "fsdp"), "ctx", None),
            P(("seq", "fsdp"), "ctx", None),
            P("fsdp", None),
            P("fsdp", None),
            P("fsdp", None),
            P("fsdp", None),
            P("fsdp"),
            P("fsdp"),
            P("fsdp"),
            P("fsdp"),
            P("fsdp"),
            P("fsdp", None),
            P("fsdp"),
            P("fsdp", None),
            P("fsdp"),
            P("fsdp"),
            P("fsdp"),
        ),
        check_vma=False,
    )
```

profile of v0, /device:TPU:0, one launch (start us, length us, event | category | flops | bytes accessed | tf_op | source)
XLA Modules:
  0.0 1809.2 jit_solution(1213545254661435694)
XLA Ops:
  9.5 5.8 all-gather.2
  15.4 23.6 %all-gather.20.cloned.1.call-done = bf16[768,768]{1,0:T(8,128)(2,1)} async-done(((bf16[384,768]{1,0:T(8,128)(2,1)}), bf16[768,768]{1,0:T(8,128)(2,1)}) %all-gather.20.cloned.1.call-update) | async-done | bytes 1179664 | tf_op jit(solution)/shard_map/all_gather | solution.py:89
  41.3 25.6 %all-gather.24.cloned.1.call-done = bf16[768,768]{1,0:T(8,128)(2,1)} async-done(((bf16[384,768]{1,0:T(8,128)(2,1)}), bf16[768,768]{1,0:T(8,128)(2,1)}) %all-gather.24.cloned.1.call-update) | async-done | bytes 1179664 | tf_op jit(solution)/shard_map/all_gather | solution.py:88
  77.4 5.9 all-gather.7
  83.3 5.8 all-gather.4
  106.9 5.8 all-gather.9
  112.8 5.8 all-gather.10
  120.5 150.1 %all-gather.32.cloned.1.call-done = bf16[4096,768]{1,0:T(8,128)(2,1)} async-done(((bf16[128,768]{1,0:T(8,128)(2,1)}), bf16[4096,768]{1,0:T(8,128)(2,1)}) %all-gather.32.cloned.1.call-update) | async-done | bytes 6291472 | tf_op jit(solution)/shard_map/all_gather | solution.py:103
  270.5 8.7 copy.44
  279.2 166.5 %all-gather.34.cloned.1.call-done = bf16[4096,768]{1,0:T(8,128)(2,1)} async-done(((bf16[128,768]{1,0:T(8,128)(2,1)}), bf16[4096,768]{1,0:T(8,128)(2,1)}) %all-gather.34.cloned.1.call-update) | async-done | bytes 6291472 | tf_op jit(solution)/shard_map/all_gather | solution.py:102
  445.8 8.6 copy.46
  454.4 33.8 %while.26 = (s32[]{:T(128)}, bf16[6,1,128,128]{2,3,1,0:T(8,128)(2,1)S(1)}, f32[6,1,2,128]{3,2,1,0:T(2,128)S(1)}, s32[6]{0:T(128)S(1)}, bf16[1,4096,768]{1,2,0:T(...) while((s32[]{:T(128)}, ...), condition=%wide.region_3.4_spmd, body=%wide.region_0.3_spmd.sunk | while | flops 275775232 | bytes 19079360 | solution.py:120
  490.3 49.7 %all-gather.28.cloned.1.call-done = bf16[768,3072]{1,0:T(8,128)(2,1)} async-done(((bf16[384,3072]{1,0:T(8,128)(2,1)}), bf16[768,3072]{1,0:T(8,128)(2,1)}) %all-gather.28.cloned.1.call-update) | async-done | bytes 4718608 | tf_op jit(solution)/shard_map/all_gather | solution.py:126
  540.0 8.4 multiply_convert_fusion.1
  548.4 59.5 %all-gather.30.cloned.1.call-done = bf16[3072,768]{1,0:T(8,128)(2,1)} async-done(((bf16[1536,768]{1,0:T(8,128)(2,1)}), bf16[3072,768]{1,0:T(8,128)(2,1)}) %all-gather.30.cloned.1.call-update) | async-done | bytes 4718608 | tf_op jit(solution)/shard_map/all_gather | solution.py:128
  619.1 72.0 %while.27 = (s32[]{:T(128)}, bf16[6,1,128,128]{2,3,1,0:T(8,128)(2,1)S(1)}, bf16[6,1,4096,128]{2,3,1,0:T(8,128)(2,1)}, bf16[6,1,4096,128]{2,3,1,0:T(8,128)(2,1)},...) while((s32[]{:T(128)}, ...), condition=%wide.region_14.15_spmd, body=%wide.region_12.14_spmd.sunk | while | flops 680558336 | bytes 47093020 | solution.py:186
  691.1 27.8 %copy.54 = bf16[6,1,4096,128]{3,1,0,2:T(2,128)(2,1)} copy(bf16[6,1,4096,128]{2,3,1,0:T(8,128)(2,1)} %get-tuple-element.112) | data formatting | bytes 12582912
  718.9 110.1 %bitcast_reduce_fusion.1 = bf16[4096,6,128]{2,1,0:T(8,128)(2,1)} fusion(bf16[6,1,4096,128]{3,1,0,2:T(2,128)(2,1)} %copy.54), kind=kLoop, calls=%fused_computation.29 | loop fusion | bytes 12582912
  829.1 7.6 copy.172
  836.8 27.9 %copy.56 = bf16[6,1,4096,128]{3,1,0,2:T(2,128)(2,1)} copy(bf16[6,1,4096,128]{2,3,1,0:T(8,128)(2,1)} %get-tuple-element.113) | data formatting | bytes 12582912
  864.6 110.0 %bitcast_reduce_fusion = bf16[4096,6,128]{2,1,0:T(8,128)(2,1)} fusion(bf16[6,1,4096,128]{3,1,0,2:T(2,128)(2,1)} %copy.56), kind=kLoop, calls=%fused_computation.28 | loop fusion | bytes 12582912
  974.6 7.7 copy.171
  995.5 21.0 %reduce-scatter.25.cloned.1.call-done = bf16[128,768]{1,0:T(8,128)(2,1)} async-done(((bf16[4096,768]{1,0:T(8,128)(2,1)}), bf16[128,768]{1,0:T(8,128)(2,1)}) %reduce-scatter.25.cloned.1.call-update) | async-done | bytes 196624
  1020.3 176.3 %reduce-scatter.27.cloned.1.call-done = bf16[128,768]{1,0:T(8,128)(2,1)} async-done(((bf16[4096,768]{1,0:T(8,128)(2,1)}), bf16[128,768]{1,0:T(8,128)(2,1)}) %reduce-scatter.27.cloned.1.call-update) | async-done | bytes 196624
  1203.8 18.1 reduce-scatter.29.cloned.1.call-done
  1223.3 26.8 %reduce-scatter.19.cloned.1.call-done = bf16[384,768]{1,0:T(8,128)(2,1)} async-done(((bf16[768,768]{1,0:T(8,128)(2,1)}), bf16[384,768]{1,0:T(8,128)(2,1)}) %reduce-scatter.19.cloned.1.call-update) | async-done | bytes 589840 | tf_op jit(solution)/shard_map/reduce_scatter | solution.py:235
  1250.1 66.5 %reduce-scatter.21.cloned.1.call-done = bf16[384,3072]{1,0:T(8,128)(2,1)} async-done(((bf16[768,3072]{1,0:T(8,128)(2,1)}), bf16[384,3072]{1,0:T(8,128)(2,1)}) %reduce-scatter.21.cloned.1.call-update) | async-done | bytes 2359312 | tf_op jit(solution)/shard_map/reduce_scatter | solution.py:253
  1316.5 66.5 %reduce-scatter.23.cloned.1.call-done = bf16[1536,768]{1,0:T(8,128)(2,1)} async-done(((bf16[3072,768]{1,0:T(8,128)(2,1)}), bf16[1536,768]{1,0:T(8,128)(2,1)}) %reduce-scatter.23.cloned.1.call-update) | async-done | bytes 2359312 | tf_op jit(solution)/shard_map/reduce_scatter | solution.py:259
  1383.2 8.6 all-reduce.10
  1395.3 15.8 reduce-scatter.31.cloned.1.call-done
  1412.4 26.8 %reduce-scatter.33.cloned.1.call-done = bf16[384,768]{1,0:T(8,128)(2,1)} async-done(((bf16[768,768]{1,0:T(8,128)(2,1)}), bf16[384,768]{1,0:T(8,128)(2,1)}) %reduce-scatter.33.cloned.1.call-update) | async-done | bytes 589840
  1440.6 356.2 %all-reduce.12 = (f32[384,768]{0,1:T(8,128)}, f32[384,768]{0,1:T(8,128)}, f32[384,768]{0,1:T(8,128)S(1)}, f32[384,768]{1,0:T(8,128)}, f32[384]{0:T(512)}, /*inde...) all-reduce(bf16[384,768]{0,1:T(8,128)(2,1)S(1)} %copy.59, ...), channel_id=1, replica_groups=mesh['ctx'=32,'seq'=2,'fsdp'=2] {'ctx','seq'}, use_global_device_ids=true, to_apply=%region_18.19 | all-reduce | flops 3543552 | bytes 21270528 | tf_op jit(solution)/shard_map/psum | solution.py:272
  (351 shorter events, 180.4 us)
Async XLA Ops:
  7.2 31.8 %copy-start = (bf16[1,128,768]{2,1,0:T(8,128)(2,1)S(1)}, bf16[1,128,768]{2,1,0:T(8,128)(2,1)}, u32[]{:S(2)}) copy-start(bf16[1,128,768]{2,1,0:T(8,128)(2,1)} %param.21) | copy-start | bytes 589828
  7.2 31.8 %all-gather.20.cloned.1.call-start = ((), (), s32[]{:S(2)}) async-start(), calls=%async_computation.8 | async-start | bytes 1769472 | tf_op jit(solution)/shard_map/all_gather | solution.py:89
  7.9 59.0 %all-gather.24.cloned.1.call-start = ((), (), s32[]{:S(2)}) async-start(), calls=%async_computation.10 | async-start | bytes 1769472 | tf_op jit(solution)/shard_map/all_gather | solution.py:88
  8.7 110.0 %all-gather.22.cloned.1.call-start = ((), (), s32[]{:S(2)}) async-start(), calls=%async_computation.9 | async-start | bytes 1769472 | tf_op jit(solution)/shard_map/all_gather | solution.py:87
  9.4 261.1 %all-gather.32.cloned.1.call-start = ((), (), s32[]{:S(2)}) async-start(), calls=%async_computation.17 | async-start | bytes 6488064 | tf_op jit(solution)/shard_map/all_gather | solution.py:103
  41.3 404.5 %all-gather.34.cloned.1.call-start = ((), (), s32[]{:S(2)}) async-start(), calls=%async_computation.18 | async-start | bytes 6488064 | tf_op jit(solution)/shard_map/all_gather | solution.py:102
  69.2 419.0 %all-gather.26.cloned.1.call-start = ((), (), s32[]{:S(2)}) async-start(), calls=%async_computation.11 | async-start | bytes 1769472 | tf_op jit(solution)/shard_map/all_gather | solution.py:90
  69.8 470.2 %all-gather.28.cloned.1.call-start = ((), (), s32[]{:S(2)}) async-start(), calls=%async_computation.12 | async-start | bytes 7077888 | tf_op jit(solution)/shard_map/all_gather | solution.py:126
  70.6 6.8 copy-start.16
  70.6 12.7 copy-start.19
  70.6 18.6 %copy-start.20 = (bf16[384]{0:T(512)(128)(2,1)S(1)}, bf16[384]{0:T(512)(128)(2,1)}, u32[]{:S(2)}) copy-start(bf16[384]{0:T(512)(128)(2,1)} %param.27) | copy-start | bytes 2308
  70.6 24.5 %copy-start.21 = (bf16[384]{0:T(512)(128)(2,1)S(1)}, bf16[384]{0:T(512)(128)(2,1)}, u32[]{:S(2)}) copy-start(bf16[384]{0:T(512)(128)(2,1)} %param.31) | copy-start | bytes 2308
  70.6 30.3 %copy-start.22 = (bf16[384]{0:T(512)(128)(2,1)S(1)}, bf16[384]{0:T(512)(128)(2,1)}, u32[]{:S(2)}) copy-start(bf16[384]{0:T(512)(128)(2,1)} %param.30) | copy-start | bytes 2308
  70.6 36.2 %copy-start.23 = (bf16[384]{0:T(512)(128)(2,1)S(1)}, bf16[384]{0:T(512)(128)(2,1)}, u32[]{:S(2)}) copy-start(bf16[384]{0:T(512)(128)(2,1)} %param.36) | copy-start | bytes 2308
  70.6 42.1 %copy-start.24 = (bf16[384]{0:T(512)(128)(2,1)S(1)}, bf16[384]{0:T(512)(128)(2,1)}, u32[]{:S(2)}) copy-start(bf16[384]{0:T(512)(128)(2,1)} %param.37) | copy-start | bytes 2308
  70.7 537.2 %all-gather.30.cloned.1.call-start = ((), (), s32[]{:S(2)}) async-start(), calls=%async_computation.13 | async-start | bytes 7077888 | tf_op jit(solution)/shard_map/all_gather | solution.py:128
  71.4 945.1 %reduce-scatter.25.cloned.1.call-start = ((), (), s32[]{:S(2)}) async-start(), calls=%async_computation.19 | async-start | bytes 6488064
  488.2 60.2 %copy-start.7 = (bf16[6,1,128,128]{2,3,1,0:T(8,128)(2,1)}, bf16[6,1,128,128]{2,3,1,0:T(8,128)(2,1)S(1)}, u32[]{:S(2)}) copy-start(bf16[6,1,128,128]{2,3,1,0:T(8,128)(2,1)S(1)} %get-tuple-element.109) | copy-start | bytes 589828
  607.8 4.7 slice-start.2
  607.8 4.7 slice-start.3
  607.8 4.7 copy-start.27
  836.7 359.9 %reduce-scatter.27.cloned.1.call-start = ((), (), s32[]{:S(2)}) async-start(), calls=%async_computation.20 | async-start | bytes 6488064
  982.3 239.6 %reduce-scatter.29.cloned.1.call-start = ((), (), s32[]{:S(2)}) async-start(), calls=%async_computation.21 | async-start | bytes 1769472
  986.3 263.8 %reduce-scatter.19.cloned.1.call-start = ((), (), s32[]{:S(2)}) async-start(), calls=%async_computation.14 | async-start | bytes 1769472 | tf_op jit(solution)/shard_map/reduce_scatter | solution.py:235
  988.0 328.5 %reduce-scatter.21.cloned.1.call-start = ((), (), s32[]{:S(2)}) async-start(), calls=%async_computation.15 | async-start | bytes 7077888 | tf_op jit(solution)/shard_map/reduce_scatter | solution.py:253
  991.8 391.2 %reduce-scatter.23.cloned.1.call-start = ((), (), s32[]{:S(2)}) async-start(), calls=%async_computation.16 | async-start | bytes 7077888 | tf_op jit(solution)/shard_map/reduce_scatter | solution.py:259
  995.5 415.5 %reduce-scatter.31.cloned.1.call-start = ((), (), s32[]{:S(2)}) async-start(), calls=%async_computation.22 | async-start | bytes 1769472
  1020.3 418.9 %reduce-scatter.33.cloned.1.call-start = ((), (), s32[]{:S(2)}) async-start(), calls=%async_computation.23 | async-start | bytes 1769472
  1198.9 3.6 copy-start.3
  1202.5 189.9 %copy-start.2 = (bf16[768,768]{1,0:T(8,128)(2,1)S(1)}, bf16[768,768]{1,0:T(8,128)(2,1)}, u32[]{:S(2)}) copy-start(bf16[768,768]{1,0:T(8,128)(2,1)} %all-gather.24.cloned.1.call-done) | copy-start | bytes 3538948
  1203.8 188.7 %copy-start.10 = (bf16[6,1,128,128]{2,3,1,0:T(8,128)(2,1)S(1)}, bf16[6,1,128,128]{2,3,1,0:T(8,128)(2,1)}, u32[]{:S(2)}) copy-start(bf16[6,1,128,128]{2,3,1,0:T(8,128)(2,1)} %copy-done.9) | copy-start | bytes 589828
  1203.8 190.2 %copy-start.1 = (bf16[768,768]{1,0:T(8,128)(2,1)S(1)}, bf16[768,768]{1,0:T(8,128)(2,1)}, u32[]{:S(2)}) copy-start(bf16[768,768]{1,0:T(8,128)(2,1)} %all-gather.20.cloned.1.call-done) | copy-start | bytes 3538948
  (26 other events, 44.7 us)
Sparse Core Ops, SparseCore 0:
  9.7 29.2 all-gather.19
  40.6 26.2 all-gather.23
  68.6 26.3 all-gather.21
  97.1 173.4 all-gather.31
  272.6 173.1 all-gather.33
  447.3 24.7 all-gather.25
  473.7 66.2 all-gather.27
  541.6 66.1 all-gather.29
  836.8 179.6 reduce-scatter.24
  1018.8 177.7 reduce-scatter.26
  1199.5 22.3 reduce-scatter.28
  1224.8 25.2 reduce-scatter.18
  1253.0 63.4 reduce-scatter.20
  1319.5 63.4 reduce-scatter.22
  1385.8 25.2 reduce-scatter.30
  1413.9 25.2 reduce-scatter.32
where the time goes:
time: 1820 us; the launch traced here: 1810 us
  waiting for transfers between devices  897 us (49%)
  blocking collectives  417 us (23%)
  local copies, waits for them, and re-layouts  382 us (21%)
  matrix products  74.2 us (4%)
    psum x1, blocking collectives, local(): lax.psum((query_matrix, keys_matrix, value_matrix, output_matrix, query_b...  356 us
    unnamed x89, local copies, waits for them, and re-layouts  312 us
    unnamed x21, waiting for transfers between devices  262 us
    all_gather x1, waiting for transfers between devices, local(): lax.all_gather(keys, 'ctx', axis=1, tiled=True)  167 us
    all_gather x1, waiting for transfers between devices, local(): lax.all_gather(values, 'ctx', axis=1, tiled=True)  150 us
    reduce_scatter x1, waiting for transfers between devices, local(): lax.psum_scatter(outer_matrix.astype(jnp.bfloat16), 'fsdp', scatter_dimen...  66.5 us
    reduce_scatter x1, waiting for transfers between devices, local(): lax.psum_scatter(inner_matrix.astype(jnp.bfloat16), 'fsdp', scatter_dimen...  66.5 us
    all_gather x1, waiting for transfers between devices, local(): lax.all_gather(w_outer, 'fsdp', axis=0, tiled=True)  59.5 us
  transfers between devices with their start and end apart: 16, of which 14 were waited for; matrix products, arithmetic and copies ran while one was open for 13% of the time, Pallas kernels for 0%

commit v1 on v0

--- a/solution.py
+++ b/solution.py
@@ -100,7 +100,9 @@
     values = (product(flat, w_value) + b_value).astype(jnp.bfloat16).reshape(seqs, block, width)
     keys_all, values_all = (
         lax.all_gather(keys, "ctx", axis=1, tiled=True),
-        lax.all_gather(values, "ctx", axis=1, tiled=True),
+        jnp.concatenate(
+            lax.all_to_all(jnp.stack([values] * lax.axis_size("ctx")), "ctx", 0, 0), axis=1
+        ),
     )
 
     def forward_group(index):

time: 1820 us -> 1700 us (0.934)
  waiting for transfers between devices: 897 us -> 649 us
  blocking collectives: 417 us -> 530 us
    all_gather x1 -> x0, waiting for transfers between devices: 150 us -> none  [local(): lax.all_gather(values, 'ctx', axis=1, tiled=True)]
    all_gather x1, blocking collectives: 5.83 us -> 118 us  [local(): lax.all_gather(b_outer, 'fsdp', axis=0, tiled=True)]
    all_gather x1, waiting for transfers between devices: 167 us -> 69.2 us  [local(): lax.all_gather(keys, 'ctx', axis=1, tiled=True)]
    unnamed x21 -> x20, waiting for transfers between devices: 262 us -> 262 us
    unnamed x89 -> x91, local copies, waits for them, and re-layouts: 312 us -> 312 us
  transfers between devices with their start and end apart: 16 -> 16, of which waited for: 14 -> 13; matrix products, arithmetic and copies ran while one was open for 13% -> 15% of each run, Pallas kernels for 0% -> 0%
where the time goes in v1:
time: 1700 us; the launch traced here: 1690 us
  waiting for transfers between devices  649 us (38%)
  blocking collectives  530 us (31%)
  local copies, waits for them, and re-layouts  395 us (23%)
  matrix products  73.7 us (4%)
    psum x1, blocking collectives, local(): lax.psum((query_matrix, keys_matrix, value_matrix, output_matrix, query_b...  356 us
    unnamed x91, local copies, waits for them, and re-layouts  312 us
    unnamed x20, waiting for transfers between devices  262 us
    all_gather x1, blocking collectives, local(): lax.all_gather(b_outer, 'fsdp', axis=0, tiled=True)  118 us
    all_gather x1, waiting for transfers between devices, local(): lax.all_gather(keys, 'ctx', axis=1, tiled=True)  69.2 us
    reduce_scatter x1, waiting for transfers between devices, local(): lax.psum_scatter(outer_matrix.astype(jnp.bfloat16), 'fsdp', scatter_dimen...  66.6 us
    reduce_scatter x1, waiting for transfers between devices, local(): lax.psum_scatter(inner_matrix.astype(jnp.bfloat16), 'fsdp', scatter_dimen...  66.3 us
    all_gather x1, waiting for transfers between devices, local(): lax.all_gather(w_outer, 'fsdp', axis=0, tiled=True)  59.5 us
  transfers between devices with their start and end apart: 16, of which 13 were waited for; matrix products, arithmetic and copies ran while one was open for 15% of the time, Pallas kernels for 0%

profile of v1, /device:TPU:0, one launch (start us, length us, event | category | flops | bytes accessed | tf_op | source)
XLA Modules:
  0.0 1694.4 jit_solution(1911568244248455209)
XLA Ops:
  9.5 29.5 %all-gather.22.cloned.1.call-done = bf16[768,768]{1,0:T(8,128)(2,1)} async-done(((bf16[384,768]{1,0:T(8,128)(2,1)}), bf16[768,768]{1,0:T(8,128)(2,1)}) %all-gather.22.cloned.1.call-update) | async-done | bytes 1179664 | tf_op jit(solution)/shard_map/all_gather | solution.py:88
  47.8 19.2 %all-gather.18.cloned.1.call-done = bf16[768,768]{1,0:T(8,128)(2,1)} async-done(((bf16[384,768]{1,0:T(8,128)(2,1)}), bf16[768,768]{1,0:T(8,128)(2,1)}) %all-gather.18.cloned.1.call-update) | async-done | bytes 1179664 | tf_op jit(solution)/shard_map/all_gather | solution.py:89
  72.8 7.4 all-to-all-start
  81.7 118.3 %all-gather.7 = bf16[2,1,384]{2,1,0:T(2,128)(2,1)S(1)} all-gather(bf16[1,1,384]{2,1,0:T(2,128)(2,1)S(1)} %reshape.272), channel_id=1, replica_groups=mesh['ctx'=32,'seq'=2,'fsdp'=2] {'fsdp'}, dimensions={0}, use_global_device_ids=true | all-gather | bytes 2304 | tf_op jit(solution)/shard_map/all_gather | solution.py:131
  200.0 5.9 all-gather.6
  229.5 5.8 all-gather.8
  235.4 6.0 all-gather.9
  243.3 8.6 copy.53
  251.9 8.8 copy.54
  260.7 69.2 %all-gather.30.cloned.1.call-done = bf16[4096,768]{1,0:T(8,128)(2,1)} async-done(((bf16[128,768]{1,0:T(8,128)(2,1)}), bf16[4096,768]{1,0:T(8,128)(2,1)}) %all-gather.30.cloned.1.call-update) | async-done | bytes 6291472 | tf_op jit(solution)/shard_map/all_gather | solution.py:102
  329.8 8.6 copy.56
  338.5 33.6 %while.26 = (s32[]{:T(128)}, bf16[6,1,128,128]{2,3,1,0:T(8,128)(2,1)S(1)}, f32[6,1,2,128]{3,2,1,0:T(2,128)S(1)}, s32[6]{0:T(128)S(1)}, bf16[1,4096,768]{1,2,0:T(...) while((s32[]{:T(128)}, ...), condition=%wide.region_3.4_spmd, body=%wide.region_0.3_spmd.sunk | while | flops 275775232 | bytes 19079360 | solution.py:122
  374.3 49.1 %all-gather.26.cloned.1.call-done = bf16[768,3072]{1,0:T(8,128)(2,1)} async-done(((bf16[384,3072]{1,0:T(8,128)(2,1)}), bf16[768,3072]{1,0:T(8,128)(2,1)}) %all-gather.26.cloned.1.call-update) | async-done | bytes 4718608 | tf_op jit(solution)/shard_map/all_gather | solution.py:128
  423.4 8.4 multiply_convert_fusion.1
  431.7 59.5 %all-gather.28.cloned.1.call-done = bf16[3072,768]{1,0:T(8,128)(2,1)} async-done(((bf16[1536,768]{1,0:T(8,128)(2,1)}), bf16[3072,768]{1,0:T(8,128)(2,1)}) %all-gather.28.cloned.1.call-update) | async-done | bytes 4718608 | tf_op jit(solution)/shard_map/all_gather | solution.py:130
  502.5 71.9 %while.27 = (s32[]{:T(128)}, bf16[6,1,128,128]{2,3,1,0:T(8,128)(2,1)S(1)}, bf16[6,1,4096,128]{2,3,1,0:T(8,128)(2,1)}, bf16[6,1,4096,128]{2,3,1,0:T(8,128)(2,1)},...) while((s32[]{:T(128)}, ...), condition=%wide.region_14.15_spmd, body=%wide.region_12.14_spmd.sunk | while | flops 680558336 | bytes 47093020 | solution.py:188
  574.4 27.9 %copy.64 = bf16[6,1,4096,128]{3,1,0,2:T(2,128)(2,1)} copy(bf16[6,1,4096,128]{2,3,1,0:T(8,128)(2,1)} %get-tuple-element.112) | data formatting | bytes 12582912
  602.2 110.3 %bitcast_reduce_fusion.1 = bf16[4096,6,128]{2,1,0:T(8,128)(2,1)} fusion(bf16[6,1,4096,128]{3,1,0,2:T(2,128)(2,1)} %copy.64), kind=kLoop, calls=%fused_computation.29 | loop fusion | bytes 12582912
  712.5 7.7 copy.182
  720.3 27.9 %copy.66 = bf16[6,1,4096,128]{3,1,0,2:T(2,128)(2,1)} copy(bf16[6,1,4096,128]{2,3,1,0:T(8,128)(2,1)} %get-tuple-element.113) | data formatting | bytes 12582912
  748.2 109.9 %bitcast_reduce_fusion = bf16[4096,6,128]{2,1,0:T(8,128)(2,1)} fusion(bf16[6,1,4096,128]{3,1,0,2:T(2,128)(2,1)} %copy.66), kind=kLoop, calls=%fused_computation.28 | loop fusion | bytes 12582912
  858.1 7.7 copy.181
  879.0 21.7 %reduce-scatter.25.cloned.1.call-done = bf16[128,768]{1,0:T(8,128)(2,1)} async-done(((bf16[4096,768]{1,0:T(8,128)(2,1)}), bf16[128,768]{1,0:T(8,128)(2,1)}) %reduce-scatter.25.cloned.1.call-update) | async-done | bytes 196624
  904.5 177.1 %reduce-scatter.27.cloned.1.call-done = bf16[128,768]{1,0:T(8,128)(2,1)} async-done(((bf16[4096,768]{1,0:T(8,128)(2,1)}), bf16[128,768]{1,0:T(8,128)(2,1)}) %reduce-scatter.27.cloned.1.call-update) | async-done | bytes 196624
  1088.8 18.3 %reduce-scatter.29.cloned.1.call-done = bf16[384,768]{1,0:T(8,128)(2,1)} async-done(((bf16[768,768]{1,0:T(8,128)(2,1)}), bf16[384,768]{1,0:T(8,128)(2,1)}) %reduce-scatter.29.cloned.1.call-update) | async-done | bytes 589840
  1108.4 26.9 %reduce-scatter.19.cloned.1.call-done = bf16[384,768]{1,0:T(8,128)(2,1)} async-done(((bf16[768,768]{1,0:T(8,128)(2,1)}), bf16[384,768]{1,0:T(8,128)(2,1)}) %reduce-scatter.19.cloned.1.call-update) | async-done | bytes 589840 | tf_op jit(solution)/shard_map/reduce_scatter | solution.py:237
  1135.4 66.3 %reduce-scatter.21.cloned.1.call-done = bf16[384,3072]{1,0:T(8,128)(2,1)} async-done(((bf16[768,3072]{1,0:T(8,128)(2,1)}), bf16[384,3072]{1,0:T(8,128)(2,1)}) %reduce-scatter.21.cloned.1.call-update) | async-done | bytes 2359312 | tf_op jit(solution)/shard_map/reduce_scatter | solution.py:255
  1201.7 66.6 %reduce-scatter.23.cloned.1.call-done = bf16[1536,768]{1,0:T(8,128)(2,1)} async-done(((bf16[3072,768]{1,0:T(8,128)(2,1)}), bf16[1536,768]{1,0:T(8,128)(2,1)}) %reduce-scatter.23.cloned.1.call-update) | async-done | bytes 2359312 | tf_op jit(solution)/shard_map/reduce_scatter | solution.py:261
  1269.4 8.6 all-reduce.10
  1281.7 14.6 reduce-scatter.31.cloned.1.call-done
  1297.7 26.8 %reduce-scatter.33.cloned.1.call-done = bf16[384,768]{1,0:T(8,128)(2,1)} async-done(((bf16[768,768]{1,0:T(8,128)(2,1)}), bf16[384,768]{1,0:T(8,128)(2,1)}) %reduce-scatter.33.cloned.1.call-update) | async-done | bytes 589840
  1325.9 356.2 %all-reduce.12 = (f32[384,768]{0,1:T(8,128)}, f32[384,768]{0,1:T(8,128)}, f32[384,768]{0,1:T(8,128)S(1)}, f32[384,768]{1,0:T(8,128)}, f32[384]{0:T(512)}, /*inde...) all-reduce(bf16[384,768]{0,1:T(8,128)(2,1)S(1)} %copy.69, ...), channel_id=1, replica_groups=mesh['ctx'=32,'seq'=2,'fsdp'=2] {'ctx','seq'}, use_global_device_ids=true, to_apply=%region_18.19 | all-reduce | flops 3543552 | bytes 21270528 | tf_op jit(solution)/shard_map/psum | solution.py:274
  (355 shorter events, 190.7 us)
Async XLA Ops:
  7.2 31.8 %copy-start = (bf16[1,128,768]{2,1,0:T(8,128)(2,1)S(1)}, bf16[1,128,768]{2,1,0:T(8,128)(2,1)}, u32[]{:S(2)}) copy-start(bf16[1,128,768]{2,1,0:T(8,128)(2,1)} %param.21) | copy-start | bytes 589828
  7.2 31.8 %all-gather.22.cloned.1.call-start = ((), (), s32[]{:S(2)}) async-start(), calls=%async_computation.11 | async-start | bytes 1769472 | tf_op jit(solution)/shard_map/all_gather | solution.py:88
  7.9 59.0 %all-gather.18.cloned.1.call-start = ((), (), s32[]{:S(2)}) async-start(), calls=%async_computation.9 | async-start | bytes 1769472 | tf_op jit(solution)/shard_map/all_gather | solution.py:89
  8.7 33.2 %copy-start.18 = (bf16[384]{0:T(512)(128)(2,1)S(1)}, bf16[384]{0:T(512)(128)(2,1)}, u32[]{:S(2)}) copy-start(bf16[384]{0:T(512)(128)(2,1)} %param.28) | copy-start | bytes 2308
  8.7 232.8 %all-gather.20.cloned.1.call-start = ((), (), s32[]{:S(2)}) async-start(), calls=%async_computation.10 | async-start | bytes 1769472 | tf_op jit(solution)/shard_map/all_gather | solution.py:87
  9.4 320.4 %all-gather.30.cloned.1.call-start = ((), (), s32[]{:S(2)}) async-start(), calls=%async_computation.18 | async-start | bytes 6488064 | tf_op jit(solution)/shard_map/all_gather | solution.py:102
  41.3 330.9 %all-gather.24.cloned.1.call-start = ((), (), s32[]{:S(2)}) async-start(), calls=%async_computation.12 | async-start | bytes 1769472 | tf_op jit(solution)/shard_map/all_gather | solution.py:90
  72.8 170.5 %all-to-all-start = ((bf16[32,1,128,768]{2,3,1,0:T(8,128)(2,1)}), bf16[32,1,128,768]{2,3,1,0:T(8,128)(2,1)}, u32[]{:S(2)}, u32[]{:S(2)}) async-start(bf16[32,1,128,768]{2,3,1,0:T(8,128)(2,1)} %stack.3), calls=%async_computation | async-start | bytes 12582912 | tf_op jit(solution)/shard_map/all_to_all | solution.py:104
  80.2 343.2 %all-gather.26.cloned.1.call-start = ((), (), s32[]{:S(2)}) async-start(), calls=%async_computation.13 | async-start | bytes 7077888 | tf_op jit(solution)/shard_map/all_gather | solution.py:128
  80.7 119.3 %copy-start.17 = (bf16[1536]{0:T(1024)(128)(2,1)S(1)}, bf16[1536]{0:T(1024)(128)(2,1)}, u32[]{:S(2)}) copy-start(bf16[1536]{0:T(1024)(128)(2,1)} %param.33) | copy-start | bytes 9220
  80.8 125.1 %copy-start.20 = (bf16[384]{0:T(512)(128)(2,1)S(1)}, bf16[384]{0:T(512)(128)(2,1)}, u32[]{:S(2)}) copy-start(bf16[384]{0:T(512)(128)(2,1)} %param.29) | copy-start | bytes 2308
  80.8 131.0 %copy-start.21 = (bf16[384]{0:T(512)(128)(2,1)S(1)}, bf16[384]{0:T(512)(128)(2,1)}, u32[]{:S(2)}) copy-start(bf16[384]{0:T(512)(128)(2,1)} %param.27) | copy-start | bytes 2308
  80.8 136.9 %copy-start.22 = (bf16[384]{0:T(512)(128)(2,1)S(1)}, bf16[384]{0:T(512)(128)(2,1)}, u32[]{:S(2)}) copy-start(bf16[384]{0:T(512)(128)(2,1)} %param.31) | copy-start | bytes 2308
  80.8 142.8 %copy-start.23 = (bf16[384]{0:T(512)(128)(2,1)S(1)}, bf16[384]{0:T(512)(128)(2,1)}, u32[]{:S(2)}) copy-start(bf16[384]{0:T(512)(128)(2,1)} %param.30) | copy-start | bytes 2308
  80.8 148.7 %copy-start.24 = (bf16[384]{0:T(512)(128)(2,1)S(1)}, bf16[384]{0:T(512)(128)(2,1)}, u32[]{:S(2)}) copy-start(bf16[384]{0:T(512)(128)(2,1)} %param.36) | copy-start | bytes 2308
  80.8 154.6 %copy-start.25 = (bf16[384]{0:T(512)(128)(2,1)S(1)}, bf16[384]{0:T(512)(128)(2,1)}, u32[]{:S(2)}) copy-start(bf16[384]{0:T(512)(128)(2,1)} %param.37) | copy-start | bytes 2308
  80.8 410.3 %all-gather.28.cloned.1.call-start = ((), (), s32[]{:S(2)}) async-start(), calls=%async_computation.14 | async-start | bytes 7077888 | tf_op jit(solution)/shard_map/all_gather | solution.py:130
  81.6 819.1 %reduce-scatter.25.cloned.1.call-start = ((), (), s32[]{:S(2)}) async-start(), calls=%async_computation.19 | async-start | bytes 6488064
  372.2 59.6 %copy-start.9 = (bf16[6,1,128,128]{2,3,1,0:T(8,128)(2,1)}, bf16[6,1,128,128]{2,3,1,0:T(8,128)(2,1)S(1)}, u32[]{:S(2)}) copy-start(bf16[6,1,128,128]{2,3,1,0:T(8,128)(2,1)S(1)} %get-tuple-element.109) | copy-start | bytes 589828
  491.2 4.7 slice-start.2
  491.2 4.7 slice-start.3
  491.2 4.7 copy-start.28
  720.2 361.4 %reduce-scatter.27.cloned.1.call-start = ((), (), s32[]{:S(2)}) async-start(), calls=%async_computation.20 | async-start | bytes 6488064
  865.8 241.2 %reduce-scatter.29.cloned.1.call-start = ((), (), s32[]{:S(2)}) async-start(), calls=%async_computation.21 | async-start | bytes 1769472
  869.8 265.6 %reduce-scatter.19.cloned.1.call-start = ((), (), s32[]{:S(2)}) async-start(), calls=%async_computation.15 | async-start | bytes 1769472 | tf_op jit(solution)/shard_map/reduce_scatter | solution.py:237
  871.5 330.2 %reduce-scatter.21.cloned.1.call-start = ((), (), s32[]{:S(2)}) async-start(), calls=%async_computation.16 | async-start | bytes 7077888 | tf_op jit(solution)/shard_map/reduce_scatter | solution.py:255
  875.3 393.0 %reduce-scatter.23.cloned.1.call-start = ((), (), s32[]{:S(2)}) async-start(), calls=%async_computation.17 | async-start | bytes 7077888 | tf_op jit(solution)/shard_map/reduce_scatter | solution.py:261
  879.0 417.4 %reduce-scatter.31.cloned.1.call-start = ((), (), s32[]{:S(2)}) async-start(), calls=%async_computation.22 | async-start | bytes 1769472
  904.4 420.1 %reduce-scatter.33.cloned.1.call-start = ((), (), s32[]{:S(2)}) async-start(), calls=%async_computation.23 | async-start | bytes 1769472
  1087.5 191.1 %copy-start.1 = (bf16[768,768]{1,0:T(8,128)(2,1)S(1)}, bf16[768,768]{1,0:T(8,128)(2,1)}, u32[]{:S(2)}) copy-start(bf16[768,768]{1,0:T(8,128)(2,1)} %all-gather.22.cloned.1.call-done) | copy-start | bytes 3538948
  1088.8 191.6 %copy-start.2 = (bf16[768,768]{1,0:T(8,128)(2,1)S(1)}, bf16[768,768]{1,0:T(8,128)(2,1)}, u32[]{:S(2)}) copy-start(bf16[768,768]{1,0:T(8,128)(2,1)} %all-gather.18.cloned.1.call-done) | copy-start | bytes 3538948
  1088.8 191.7 %copy-start.8 = (bf16[6,1,128,128]{2,3,1,0:T(8,128)(2,1)S(1)}, bf16[6,1,128,128]{2,3,1,0:T(8,128)(2,1)}, u32[]{:S(2)}) copy-start(bf16[6,1,128,128]{2,3,1,0:T(8,128)(2,1)} %copy-done.7) | copy-start | bytes 589828
  (27 other events, 48.0 us)
Sparse Core Ops, SparseCore 0:
  9.7 29.2 all-gather.21
  40.6 26.2 all-gather.17
  68.6 38.4 all-gather.19
  109.2 220.6 all-gather.29
  331.3 24.2 all-gather.23
  357.1 66.1 all-gather.25
  425.0 66.1 all-gather.27
  720.4 180.2 reduce-scatter.24
  903.1 178.4 reduce-scatter.26
  1084.4 22.6 reduce-scatter.28
  1110.1 25.2 reduce-scatter.18
  1138.2 63.4 reduce-scatter.20
  1204.8 63.4 reduce-scatter.22
  1271.1 25.2 reduce-scatter.30
  1299.2 25.2 reduce-scatter.32
